TPU v7x, 512 devices: a whole 4x8x8 slice. The times are simulated.
512 devices in a mesh: row: 32 (over y_lo, x, core), col: 16 (over z, y_hi).
Axes of the slice: x: 4, y: 8 (y_hi: 2, y_lo: 4; y = y_hi * 4 + y_lo), z: 8, core: 2. Of those that a mesh axis runs over, the one named last changes fastest.
Arguments:
- features: bfloat16 [98304, 256], P(('row', 'col')), may hold values from -6 to 6
- weight: bfloat16 [256, 256], replicated, may hold values from -0.375 to 0.375
- tiles: bfloat16 [32, 16, 256, 64, 128], P('row', 'col'), may hold values from -0.0546875 to 0.0546875
- tile_rows: int32 [32, 16, 512], P('row', 'col'), may hold values from 0 to 47
- tile_cols: int32 [32, 16, 512], P('row', 'col'), may hold values from 0 to 95
- counts: int32 [32, 16], P('row', 'col'), may hold values from 128 to 512, as said below
Outputs:
- output: bfloat16 [98304, 256], P(('row', 'col'))
Inputs may be any that keep to these rules, and one draw needn't show every extreme that they name: `counts`: some grid cell has exactly 512 live slots.
All inputs are finite; a program needn't handle non-finite values.
Results may differ from a plain program's by a relative error of at most 0.0049.
Values may be sent and summed in bfloat16 or wider, within the bound.
No kernel may reach another device: no remote copies, remote signals or barrier semaphores. Data moves between devices by JAX's collectives and lax.ppermute only.
A program may use at most 64 MiB of HBM per device.

v0:
```python
import jax
import jax.numpy as jnp
from jax import lax
from jax.sharding import PartitionSpec as P

TILE = 64


def body(features, weight, tiles, tile_rows, tile_cols, counts):
    feature_width = weight.shape[1]
    product_rows = jnp.dot(features, weight, preferred_element_type=jnp.float32).astype(
        jnp.bfloat16
    )
    gathered = lax.all_gather(product_rows, "row", axis=0, tiled=True)
    column_table = gathered.reshape(gathered.shape[0] // TILE, TILE, feature_width)
    row_tiles = lax.axis_size("col") * features.shape[0] // TILE
    slot_count = tile_rows.shape[2]
    block_size = min(64, slot_count)
    half_block = block_size // 2
    passes = slot_count // block_size
    pair_list = tiles[0, 0]
    row_list = tile_rows[0, 0]
    col_list = tile_cols[0, 0]
    live_count = counts[0, 0]
    block_slots = jnp.arange(block_size, dtype=jnp.int32)

    def add_block(block_index, total):
        first = block_index * block_size
        pair_block = lax.dynamic_slice_in_dim(pair_list, block_index * half_block, half_block, 0)
        pair_block = pair_block.reshape(half_block, TILE, 2, TILE)
        row_block = lax.dynamic_slice_in_dim(row_list, first, block_size, 0)
        col_block = lax.dynamic_slice_in_dim(col_list, first, block_size, 0)
        picked = column_table[col_block].reshape(half_block, 2, TILE, feature_width)
        terms = jnp.einsum(
            "qajb,qjbf->qjaf", pair_block, picked, preferred_element_type=jnp.float32
        )
        terms = terms.reshape(block_size, TILE, feature_width)
        in_use = (first + block_slots < live_count).astype(jnp.float32)
        terms = terms * in_use[:, None, None]
        return total.at[row_block].add(terms)

    zero_total = jnp.zeros((row_tiles, TILE, feature_width), jnp.float32)
    total = lax.fori_loop(0, passes, add_block, zero_total)
    partial_value = total.reshape(row_tiles * TILE, feature_width)
    own_rows = lax.psum_scatter(partial_value, "col", scatter_dimension=0, tiled=True)
    return jnp.maximum(own_rows, 0.0).astype(jnp.bfloat16)


def solution(mesh):
    return jax.shard_map(
        body,
        mesh=mesh,
        in_specs=(
            P(("row", "col"), None),
            P(),
            P("row", "col", None, None, None),
            P("row", "col", None),
            P("row", "col", None),
            P("row", "col"),
        ),
        out_specs=P(("row", "col"), None),
        check_vma=False,
    )
```

profile of v0, /device:TPU:12, one launch (start us, length us, event | category | flops | bytes accessed | tf_op | source)
XLA Modules:
  0.0 513.0 jit_solution(17624238361777435077)
XLA Ops:
  6.5 0.9 copy-done
  7.4 1.7 convolution_convert_fusion
  9.2 67.9 %all-gather.2.cloned.1.call-done = bf16[6144,256]{1,0:T(8,128)(2,1)} async-done(((bf16[192,256]{1,0:T(8,128)(2,1)}), bf16[6144,256]{1,0:T(8,128)(2,1)}) %all-gather.2.cloned.1.call-update) | async-done | bytes 3145744 | tf_op jit(solution)/shard_map/all_gather | solution.py:14
  77.5 195.1 %while.14 = (s32[]{:T(128)}, f32[48,64,256]{2,1,0:T(8,128)S(1)}, s32[512]{0:T(512)}, bf16[256,64,128]{2,1,0:T(8,128)(2,1)}, s32[512]{0:T(512)}, /*index=5*/bf16[...) while((s32[]{:T(128)}, f32[48,64,256]{2,1,0:T(8,128)S(1)}, ...), condition=%wide.region_2.0_spmd.clone, body=%wide.region_0.0_spmd.clone.sunk | while | flops 136316496 | bytes 34085360 | solution.py:43
  77.5 0.7 compare_convert_fusion.2
  78.1 0.8 compare_select_fusion.3
  78.9 1.9 constant_dynamic-slice_fusion.2
  80.8 3.2 reshape.70
  84.0 3.9 gather_fusion
  87.9 2.6 fusion.12
  90.5 2.5 bitcast_multiply_fusion.2
  93.0 8.8 %scatter_fusion = f32[48,64,256]{2,1,0:T(8,128)S(1)} fusion(f32[48,64,256]{2,1,0:T(8,128)S(1)} %get-tuple-element.238, s32[64]{0:T(128)S(1)} %get-tuple-element.222, f32[64,64,256]{2,1,0:T(8,128)} %bitcast_multiply_fusion.2), kind=kCustom, calls=%fused_computation.1.clone.clone.1 | custom fusion | flops 1048576 | bytes 12583168 | tf_op jit(solution)/shard_map/while/body/eval_jaxpr/scatter-add | solution.py:40
  102.5 0.8 compare_select_fusion.3
  103.3 1.9 constant_dynamic-slice_fusion.2
  105.2 3.2 reshape.70
  108.4 3.9 gather_fusion
  112.3 2.6 fusion.12
  114.9 2.5 bitcast_multiply_fusion.2
  117.4 8.8 %scatter_fusion = f32[48,64,256]{2,1,0:T(8,128)S(1)} fusion(f32[48,64,256]{2,1,0:T(8,128)S(1)} %get-tuple-element.238, s32[64]{0:T(128)S(1)} %get-tuple-element.222, f32[64,64,256]{2,1,0:T(8,128)} %bitcast_multiply_fusion.2), kind=kCustom, calls=%fused_computation.1.clone.clone.1 | custom fusion | flops 1048576 | bytes 12583168 | tf_op jit(solution)/shard_map/while/body/eval_jaxpr/scatter-add | solution.py:40
  126.9 0.8 compare_select_fusion.3
  127.7 1.9 constant_dynamic-slice_fusion.2
  129.6 3.2 reshape.70
  132.8 3.9 gather_fusion
  136.7 2.6 fusion.12
  139.3 2.5 bitcast_multiply_fusion.2
  141.8 8.8 %scatter_fusion = f32[48,64,256]{2,1,0:T(8,128)S(1)} fusion(f32[48,64,256]{2,1,0:T(8,128)S(1)} %get-tuple-element.238, s32[64]{0:T(128)S(1)} %get-tuple-element.222, f32[64,64,256]{2,1,0:T(8,128)} %bitcast_multiply_fusion.2), kind=kCustom, calls=%fused_computation.1.clone.clone.1 | custom fusion | flops 1048576 | bytes 12583168 | tf_op jit(solution)/shard_map/while/body/eval_jaxpr/scatter-add | solution.py:40
  151.3 0.8 compare_select_fusion.3
  152.1 1.9 constant_dynamic-slice_fusion.2
  154.0 3.2 reshape.70
  157.2 3.9 gather_fusion
  161.1 2.6 fusion.12
  163.7 2.5 bitcast_multiply_fusion.2
  166.2 8.8 %scatter_fusion = f32[48,64,256]{2,1,0:T(8,128)S(1)} fusion(f32[48,64,256]{2,1,0:T(8,128)S(1)} %get-tuple-element.238, s32[64]{0:T(128)S(1)} %get-tuple-element.222, f32[64,64,256]{2,1,0:T(8,128)} %bitcast_multiply_fusion.2), kind=kCustom, calls=%fused_computation.1.clone.clone.1 | custom fusion | flops 1048576 | bytes 12583168 | tf_op jit(solution)/shard_map/while/body/eval_jaxpr/scatter-add | solution.py:40
  175.7 0.8 compare_select_fusion.3
  176.5 1.9 constant_dynamic-slice_fusion.2
  178.4 3.2 reshape.70
  181.6 3.9 gather_fusion
  185.4 2.6 fusion.12
  188.1 2.5 bitcast_multiply_fusion.2
  190.6 8.8 %scatter_fusion = f32[48,64,256]{2,1,0:T(8,128)S(1)} fusion(f32[48,64,256]{2,1,0:T(8,128)S(1)} %get-tuple-element.238, s32[64]{0:T(128)S(1)} %get-tuple-element.222, f32[64,64,256]{2,1,0:T(8,128)} %bitcast_multiply_fusion.2), kind=kCustom, calls=%fused_computation.1.clone.clone.1 | custom fusion | flops 1048576 | bytes 12583168 | tf_op jit(solution)/shard_map/while/body/eval_jaxpr/scatter-add | solution.py:40
  200.1 0.8 compare_select_fusion.3
  200.9 1.9 constant_dynamic-slice_fusion.2
  202.8 3.2 reshape.70
  205.9 3.9 gather_fusion
  209.8 2.6 fusion.12
  212.4 2.5 bitcast_multiply_fusion.2
  215.0 8.8 %scatter_fusion = f32[48,64,256]{2,1,0:T(8,128)S(1)} fusion(f32[48,64,256]{2,1,0:T(8,128)S(1)} %get-tuple-element.238, s32[64]{0:T(128)S(1)} %get-tuple-element.222, f32[64,64,256]{2,1,0:T(8,128)} %bitcast_multiply_fusion.2), kind=kCustom, calls=%fused_computation.1.clone.clone.1 | custom fusion | flops 1048576 | bytes 12583168 | tf_op jit(solution)/shard_map/while/body/eval_jaxpr/scatter-add | solution.py:40
  224.5 0.8 compare_select_fusion.3
  225.3 1.9 constant_dynamic-slice_fusion.2
  227.1 3.2 reshape.70
  230.3 3.9 gather_fusion
  234.2 2.6 fusion.12
  236.8 2.5 bitcast_multiply_fusion.2
  239.4 8.8 %scatter_fusion = f32[48,64,256]{2,1,0:T(8,128)S(1)} fusion(f32[48,64,256]{2,1,0:T(8,128)S(1)} %get-tuple-element.238, s32[64]{0:T(128)S(1)} %get-tuple-element.222, f32[64,64,256]{2,1,0:T(8,128)} %bitcast_multiply_fusion.2), kind=kCustom, calls=%fused_computation.1.clone.clone.1 | custom fusion | flops 1048576 | bytes 12583168 | tf_op jit(solution)/shard_map/while/body/eval_jaxpr/scatter-add | solution.py:40
  248.9 0.8 compare_select_fusion.3
  249.7 1.9 constant_dynamic-slice_fusion.2
  251.5 3.2 reshape.70
  254.7 3.9 gather_fusion
  258.6 2.6 fusion.12
  261.2 2.5 bitcast_multiply_fusion.2
  263.8 8.8 %scatter_fusion = f32[48,64,256]{2,1,0:T(8,128)S(1)} fusion(f32[48,64,256]{2,1,0:T(8,128)S(1)} %get-tuple-element.238, s32[64]{0:T(128)S(1)} %get-tuple-element.222, f32[64,64,256]{2,1,0:T(8,128)} %bitcast_multiply_fusion.2), kind=kCustom, calls=%fused_computation.1.clone.clone.1 | custom fusion | flops 1048576 | bytes 12583168 | tf_op jit(solution)/shard_map/while/body/eval_jaxpr/scatter-add | solution.py:40
  272.6 1.6 copy-done.1
  274.3 230.3 %reduce-scatter.2.cloned.1.call-done = f32[192,256]{1,0:T(8,128)} async-done(((f32[3072,256]{1,0:T(8,128)}), f32[192,256]{1,0:T(8,128)}) %reduce-scatter.2.cloned.1.call-update) | async-done | bytes 196624 | tf_op jit(solution)/shard_map/reduce_scatter | solution.py:45
  504.6 1.6 maximum_convert_fusion
  (22 shorter events, 5.0 us)
Async XLA Ops:
  6.5 0.9 copy-start
  6.5 70.6 %all-gather.2.cloned.1.call-start = ((), (), s32[]{:S(2)}) async-start(), calls=%async_computation.1 | async-start | bytes 3244032 | tf_op jit(solution)/shard_map/all_gather | solution.py:14
  9.2 495.4 %reduce-scatter.2.cloned.1.call-start = ((), (), s32[]{:S(2)}) async-start(), calls=%async_computation.2 | async-start | bytes 3342336 | tf_op jit(solution)/shard_map/reduce_scatter | solution.py:45
  272.6 1.6 copy-start.1
Sparse Core Ops, SparseCore 0:
  9.5 67.5 all-gather.1
  274.4 230.1 reduce-scatter.1
where the time goes:
time: 516 us; the launch traced here: 513 us
  waiting for transfers between devices  298 us (58%)
  other arithmetic  104 us (20%)
  local copies, waits for them, and re-layouts  74.5 us (14%)
  matrix products  22.6 us (4%)
  between operations  13.4 us (3%)
    reduce_scatter x1, waiting for transfers between devices, body(): lax.psum_scatter(partial_value, 'col', scatter_dimension=0, tiled=True)  230 us
    scatter-add x8, other arithmetic, add_block(): return total.at[row_block].add(terms)  70.4 us
    all_gather x1, waiting for transfers between devices, body(): gathered = lax.all_gather(product_rows, 'row', axis=0, tiled=True)  67.9 us
    gather x8, local copies, waits for them, and re-layouts, add_block(): picked = column_table[col_block].reshape(half_block, 2, TILE, feature_width)  31.2 us
    reshape x8, local copies, waits for them, and re-layouts, add_block(): pair_block = pair_block.reshape(half_block, TILE, 2, TILE)  25.5 us
    dot_general x8, matrix products, add_block(): jnp.einsum('qajb,qjbf->qjaf', pair_block, picked, preferred_element_type=...  20.8 us
    mul x8, other arithmetic, add_block(): terms = terms * in_use[:, None, None]  20.4 us
    dynamic_slice x8, local copies, waits for them, and re-layouts, add_block(): lax.dynamic_slice_in_dim(pair_list, block_index * half_block, half_block, 0)  14.9 us
  transfers between devices with their start and end apart: 2, of which 2 were waited for; matrix products, arithmetic and copies ran while one was open for 0% of the time, Pallas kernels for 0%

commit v1 on v0

--- a/solution.py
+++ b/solution.py
@@ -11,7 +11,9 @@
     product_rows = jnp.dot(features, weight, preferred_element_type=jnp.float32).astype(
         jnp.bfloat16
     )
-    gathered = lax.all_gather(product_rows, "row", axis=0, tiled=True)
+    gathered = jnp.concatenate(
+        lax.all_to_all(jnp.stack([product_rows] * lax.axis_size("row")), "row", 0, 0), axis=0
+    )
     column_table = gathered.reshape(gathered.shape[0] // TILE, TILE, feature_width)
     row_tiles = lax.axis_size("col") * features.shape[0] // TILE
     slot_count = tile_rows.shape[2]

time: 516 us -> 531 us (1.029)
  the two profiles are of different devices: /device:TPU:12 before, /device:TPU:10 now
where the time goes in v1:
time: 531 us; the launch traced here: 529 us
  waiting for transfers between devices  301 us (57%)
  other arithmetic  104 us (20%)
  local copies, waits for them, and re-layouts  78.2 us (15%)
  matrix products  21.9 us (4%)
  between operations  13.4 us (3%)
  starting transfers between devices  9.61 us (2%)
    reduce_scatter x1, waiting for transfers between devices, body(): lax.psum_scatter(partial_value, 'col', scatter_dimension=0, tiled=True)  233 us
    scatter-add x8, other arithmetic, add_block(): return total.at[row_block].add(terms)  70.4 us
    all_to_all x1, waiting for transfers between devices, body(): lax.all_to_all(jnp.stack([product_rows] * lax.axis_size('row')), 'row', 0...  68.3 us
    gather x8, local copies, waits for them, and re-layouts, add_block(): picked = column_table[col_block].reshape(half_block, 2, TILE, feature_width)  31.2 us
    reshape x8, local copies, waits for them, and re-layouts, add_block(): pair_block = pair_block.reshape(half_block, TILE, 2, TILE)  25.5 us
    dot_general x8, matrix products, add_block(): jnp.einsum('qajb,qjbf->qjaf', pair_block, picked, preferred_element_type=...  20.8 us
    mul x8, other arithmetic, add_block(): terms = terms * in_use[:, None, None]  20.4 us
    dynamic_slice x8, local copies, waits for them, and re-layouts, add_block(): lax.dynamic_slice_in_dim(pair_list, block_index * half_block, half_block, 0)  14.9 us
  transfers between devices with their start and end apart: 2, of which 2 were waited for; matrix products, arithmetic and copies ran while one was open for 0% of the time, Pallas kernels for 0%

profile of v1, /device:TPU:10, one launch (start us, length us, event | category | flops | bytes accessed | tf_op | source)
XLA Modules:
  0.0 528.7 jit_solution(17663666225599215256)
XLA Ops:
  6.5 0.9 copy-done
  7.4 1.1 convolution_convert_fusion
  8.5 2.0 stack.2
  10.5 9.6 %all-to-all-start = ((bf16[32,192,256]{2,1,0:T(8,128)(2,1)}), bf16[32,192,256]{2,1,0:T(8,128)(2,1)S(1)}, u32[]{:S(2)}, u32[]{:S(2)}) async-start(bf16[32,192,256]{2,1,0:T(8,128)(2,1)} %stack.2), calls=%async_computation | async-start | bytes 6291456 | tf_op jit(solution)/shard_map/all_to_all | solution.py:15
  20.1 68.3 %all-to-all-done = bf16[32,192,256]{2,1,0:T(8,128)(2,1)S(1)} async-done(((bf16[32,192,256]{2,1,0:T(8,128)(2,1)}), bf16[32,192,256]{2,1,0:T(8,128)(2,1)S(1)}, u32[]{:S(2)}, u32[]{:S(2)}) %all-to-all-start) | async-done | bytes 3145760 | tf_op jit(solution)/shard_map/all_to_all | solution.py:15
  88.4 1.7 copy-done.2
  90.5 195.1 %while.14 = (s32[]{:T(128)}, f32[48,64,256]{2,1,0:T(8,128)S(1)}, s32[512]{0:T(512)}, bf16[256,64,128]{2,1,0:T(8,128)(2,1)}, s32[512]{0:T(512)}, /*index=5*/bf16[...) while((s32[]{:T(128)}, f32[48,64,256]{2,1,0:T(8,128)S(1)}, ...), condition=%wide.region_2.0_spmd.clone, body=%wide.region_0.0_spmd.clone.sunk | while | flops 136316496 | bytes 34085360 | solution.py:45
  91.2 0.8 compare_select_fusion.3
  92.0 1.9 constant_dynamic-slice_fusion.2
  93.8 3.2 reshape.68
  97.0 3.9 gather_fusion
  100.9 2.6 fusion.12
  103.5 2.5 bitcast_multiply_fusion.2
  106.1 8.8 %scatter_fusion = f32[48,64,256]{2,1,0:T(8,128)S(1)} fusion(f32[48,64,256]{2,1,0:T(8,128)S(1)} %get-tuple-element.238, s32[64]{0:T(128)S(1)} %get-tuple-element.222, f32[64,64,256]{2,1,0:T(8,128)} %bitcast_multiply_fusion.2), kind=kCustom, calls=%fused_computation.1.clone.clone.1 | custom fusion | flops 1048576 | bytes 12583168 | tf_op jit(solution)/shard_map/while/body/eval_jaxpr/scatter-add | solution.py:42
  115.6 0.8 compare_select_fusion.3
  116.4 1.9 constant_dynamic-slice_fusion.2
  118.2 3.2 reshape.68
  121.4 3.9 gather_fusion
  125.3 2.6 fusion.12
  127.9 2.5 bitcast_multiply_fusion.2
  130.5 8.8 %scatter_fusion = f32[48,64,256]{2,1,0:T(8,128)S(1)} fusion(f32[48,64,256]{2,1,0:T(8,128)S(1)} %get-tuple-element.238, s32[64]{0:T(128)S(1)} %get-tuple-element.222, f32[64,64,256]{2,1,0:T(8,128)} %bitcast_multiply_fusion.2), kind=kCustom, calls=%fused_computation.1.clone.clone.1 | custom fusion | flops 1048576 | bytes 12583168 | tf_op jit(solution)/shard_map/while/body/eval_jaxpr/scatter-add | solution.py:42
  140.0 0.8 compare_select_fusion.3
  140.8 1.9 constant_dynamic-slice_fusion.2
  142.6 3.2 reshape.68
  145.8 3.9 gather_fusion
  149.7 2.6 fusion.12
  152.3 2.5 bitcast_multiply_fusion.2
  154.9 8.8 %scatter_fusion = f32[48,64,256]{2,1,0:T(8,128)S(1)} fusion(f32[48,64,256]{2,1,0:T(8,128)S(1)} %get-tuple-element.238, s32[64]{0:T(128)S(1)} %get-tuple-element.222, f32[64,64,256]{2,1,0:T(8,128)} %bitcast_multiply_fusion.2), kind=kCustom, calls=%fused_computation.1.clone.clone.1 | custom fusion | flops 1048576 | bytes 12583168 | tf_op jit(solution)/shard_map/while/body/eval_jaxpr/scatter-add | solution.py:42
  164.4 0.8 compare_select_fusion.3
  165.1 1.9 constant_dynamic-slice_fusion.2
  167.0 3.2 reshape.68
  170.2 3.9 gather_fusion
  174.1 2.6 fusion.12
  176.7 2.5 bitcast_multiply_fusion.2
  179.2 8.8 %scatter_fusion = f32[48,64,256]{2,1,0:T(8,128)S(1)} fusion(f32[48,64,256]{2,1,0:T(8,128)S(1)} %get-tuple-element.238, s32[64]{0:T(128)S(1)} %get-tuple-element.222, f32[64,64,256]{2,1,0:T(8,128)} %bitcast_multiply_fusion.2), kind=kCustom, calls=%fused_computation.1.clone.clone.1 | custom fusion | flops 1048576 | bytes 12583168 | tf_op jit(solution)/shard_map/while/body/eval_jaxpr/scatter-add | solution.py:42
  188.7 0.8 compare_select_fusion.3
  189.5 1.9 constant_dynamic-slice_fusion.2
  191.4 3.2 reshape.68
  194.6 3.9 gather_fusion
  198.5 2.6 fusion.12
  201.1 2.5 bitcast_multiply_fusion.2
  203.6 8.8 %scatter_fusion = f32[48,64,256]{2,1,0:T(8,128)S(1)} fusion(f32[48,64,256]{2,1,0:T(8,128)S(1)} %get-tuple-element.238, s32[64]{0:T(128)S(1)} %get-tuple-element.222, f32[64,64,256]{2,1,0:T(8,128)} %bitcast_multiply_fusion.2), kind=kCustom, calls=%fused_computation.1.clone.clone.1 | custom fusion | flops 1048576 | bytes 12583168 | tf_op jit(solution)/shard_map/while/body/eval_jaxpr/scatter-add | solution.py:42
  213.1 0.8 compare_select_fusion.3
  213.9 1.9 constant_dynamic-slice_fusion.2
  215.8 3.2 reshape.68
  219.0 3.9 gather_fusion
  222.9 2.6 fusion.12
  225.5 2.5 bitcast_multiply_fusion.2
  228.0 8.8 %scatter_fusion = f32[48,64,256]{2,1,0:T(8,128)S(1)} fusion(f32[48,64,256]{2,1,0:T(8,128)S(1)} %get-tuple-element.238, s32[64]{0:T(128)S(1)} %get-tuple-element.222, f32[64,64,256]{2,1,0:T(8,128)} %bitcast_multiply_fusion.2), kind=kCustom, calls=%fused_computation.1.clone.clone.1 | custom fusion | flops 1048576 | bytes 12583168 | tf_op jit(solution)/shard_map/while/body/eval_jaxpr/scatter-add | solution.py:42
  238.3 1.9 constant_dynamic-slice_fusion.2
  240.2 3.2 reshape.68
  243.4 3.9 gather_fusion
  247.3 2.6 fusion.12
  249.9 2.5 bitcast_multiply_fusion.2
  252.4 8.8 %scatter_fusion = f32[48,64,256]{2,1,0:T(8,128)S(1)} fusion(f32[48,64,256]{2,1,0:T(8,128)S(1)} %get-tuple-element.238, s32[64]{0:T(128)S(1)} %get-tuple-element.222, f32[64,64,256]{2,1,0:T(8,128)} %bitcast_multiply_fusion.2), kind=kCustom, calls=%fused_computation.1.clone.clone.1 | custom fusion | flops 1048576 | bytes 12583168 | tf_op jit(solution)/shard_map/while/body/eval_jaxpr/scatter-add | solution.py:42
  262.7 1.9 constant_dynamic-slice_fusion.2
  264.6 3.2 reshape.68
  267.7 3.9 gather_fusion
  271.6 2.6 fusion.12
  274.2 2.5 bitcast_multiply_fusion.2
  276.8 8.8 %scatter_fusion = f32[48,64,256]{2,1,0:T(8,128)S(1)} fusion(f32[48,64,256]{2,1,0:T(8,128)S(1)} %get-tuple-element.238, s32[64]{0:T(128)S(1)} %get-tuple-element.222, f32[64,64,256]{2,1,0:T(8,128)} %bitcast_multiply_fusion.2), kind=kCustom, calls=%fused_computation.1.clone.clone.1 | custom fusion | flops 1048576 | bytes 12583168 | tf_op jit(solution)/shard_map/while/body/eval_jaxpr/scatter-add | solution.py:42
  285.6 1.6 copy-done.1
  287.3 233.0 %reduce-scatter.2.cloned.1.call-done = f32[192,256]{1,0:T(8,128)} async-done(((f32[3072,256]{1,0:T(8,128)}), f32[192,256]{1,0:T(8,128)}) %reduce-scatter.2.cloned.1.call-update) | async-done | bytes 196624 | tf_op jit(solution)/shard_map/reduce_scatter | solution.py:47
  520.3 1.6 maximum_convert_fusion
  (24 shorter events, 7.2 us)
Async XLA Ops:
  6.5 0.9 copy-start
  10.5 77.9 %all-to-all-start = ((bf16[32,192,256]{2,1,0:T(8,128)(2,1)}), bf16[32,192,256]{2,1,0:T(8,128)(2,1)S(1)}, u32[]{:S(2)}, u32[]{:S(2)}) async-start(bf16[32,192,256]{2,1,0:T(8,128)(2,1)} %stack.2), calls=%async_computation | async-start | bytes 6291456 | tf_op jit(solution)/shard_map/all_to_all | solution.py:15
  20.1 500.2 %reduce-scatter.2.cloned.1.call-start = ((), (), s32[]{:S(2)}) async-start(), calls=%async_computation.2 | async-start | bytes 3342336 | tf_op jit(solution)/shard_map/reduce_scatter | solution.py:47
  88.4 1.7 copy-start.2
  285.6 1.6 copy-start.1
Sparse Core Ops, SparseCore 0:
  287.4 232.8 reduce-scatter.1
